TPU v7x, 32 devices: a whole 2x2x4 slice. The times are simulated.
32 devices in a mesh: seq: 8 (over z, x), head: 2 (over y), dp: 2 (over core).
Axes of the slice: x: 2, y: 2, z: 4, core: 2. Of those that a mesh axis runs over, the one named last changes fastest.
Arguments:
- queries: bfloat16 [2, 2048, 1024], P('dp', 'seq', 'head'), may hold values from -6 to 6
- key_rows: bfloat16 [2, 2048, 1024], P('dp', 'seq', 'head'), may hold values from -6 to 6
- value_rows: bfloat16 [2, 2048, 1024], P('dp', 'seq', 'head'), may hold values from -140 to 140
- stretch_doc: int32 [2, 8], P('dp', 'seq'), may hold values from 0 to 3, never falling along the last dimension, each value on 1 to 4 neighbouring positions
- head_gain: float32 [8, 128], P('head'), may hold values from 0.1 to 1.9
- w_out: bfloat16 [1024, 2048], P('head'), may hold values from -0.1875 to 0.1875
- cotangent: bfloat16 [2, 2048, 2048], P('dp', 'seq'), may hold values from -40 to 40
Outputs:
- layer_out: bfloat16 [2, 2048, 2048], P('dp', ('seq', 'head'))
- query_grad: bfloat16 [2, 2048, 1024], P('dp', 'seq', 'head')
- key_grad: bfloat16 [2, 2048, 1024], P('dp', 'seq', 'head')
- value_grad: bfloat16 [2, 2048, 1024], P('dp', 'seq', 'head')
- gain_grad: float32 [8, 128], P('head')
Inputs may be any that keep to these rules, and one draw needn't show every extreme that they name: `stretch_doc`: document numbers never fall along a sequence; each document spans 1 to 4 whole stretches, and one spans exactly that many.
All inputs are finite; a program needn't handle non-finite values.
Results may differ from a plain program's by a relative error of at most 0.0055.
Values may be sent and summed in bfloat16 or wider, within the bound.
No kernel may reach another device: no remote copies, remote signals or barrier semaphores. Data moves between devices by JAX's collectives and lax.ppermute only.
A program may use at most 64 MiB of HBM per device.

v0:
```python
import math
import jax
import jax.numpy as jnp
from jax import lax
from jax.sharding import PartitionSpec as P

epsilon = 1e-05
highest = lax.Precision.HIGHEST


def shifted(block, axis, distance):
    devices = range(lax.axis_size(axis))
    route = [(i - distance, i) for i in devices if i - distance in devices]
    return lax.ppermute(block, axis, route)


def link_docs(earlier, following):
    sum_early, doc_early = earlier
    sum_late, doc_late = following
    merged = jnp.where(doc_early[0] == doc_late[0], sum_late + sum_early, sum_late)
    running = jnp.where(doc_late[0] < 0.5, sum_early, merged)
    return (running, jnp.where(doc_late < 0.5, doc_early, doc_late))


def double_chain(start, mover, seq_size):
    current = mover(start, 1)
    reach = 1
    while reach < seq_size - 1:
        current = link_docs(mover(current, reach), current)
        reach = reach * 2
    return current


def on_device(queries, key_rows, value_rows, stretch_doc, head_gain, w_out, cotangent):
    token_count = queries.shape[1]
    local_width = queries.shape[2]
    head_count = head_gain.shape[0]
    head_dim = head_gain.shape[1]
    stretches = stretch_doc.shape[1]
    stretch_len = token_count // stretches
    seq_size = lax.axis_size("seq")
    blocks = (stretches, stretch_len, head_count, head_dim)
    query_blk = queries[0].reshape(blocks)
    key_blk = key_rows[0].reshape(blocks)
    value_blk = value_rows[0].reshape(blocks)
    doc_ids = stretch_doc[0]
    doc_float = doc_ids.astype(jnp.float32) + 1.0
    stretch_order = jnp.arange(stretches)
    same_doc = doc_ids[:, None] == doc_ids[None, :]
    before_mask = jnp.where(
        same_doc & (stretch_order[None, :] < stretch_order[:, None]), 1.0, 0.0
    ).astype(jnp.float32)
    after_mask = jnp.where(
        same_doc & (stretch_order[None, :] > stretch_order[:, None]), 1.0, 0.0
    ).astype(jnp.float32)
    positions = jnp.arange(stretch_len)
    causal = positions[:, None] >= positions[None, :]

    def move_forward(pair, distance):
        return shifted((pair[0], pair[1]), "seq", distance)

    def move_backward(pair, distance):
        return shifted((pair[0], pair[1]), "seq", -distance)

    kv_sum = jnp.einsum("cshd,cshe->chde", key_blk, value_blk, preferred_element_type=jnp.float32)
    last_pick = jnp.where(doc_float == doc_float[0], 1.0, 0.0).astype(jnp.float32)
    own_state = jnp.einsum("c,chde->hde", last_pick, kv_sum, precision=highest)
    incoming, incoming_doc = double_chain((own_state, doc_float), move_forward, seq_size)
    take_in = jnp.where(doc_float == incoming_doc[0], 1.0, 0.0).astype(jnp.float32)
    states = (
        jnp.einsum("cj,jhde->chde", before_mask, kv_sum, precision=highest)
        + take_in[:, None, None, None] * incoming
    )
    scores = jnp.einsum("cthd,cshd->chts", query_blk, key_blk, preferred_element_type=jnp.float32)
    attn_weights = jnp.where(causal, scores, 0.0).astype(jnp.bfloat16)
    within = jnp.einsum(
        "chts,cshe->cthe", attn_weights, value_blk, preferred_element_type=jnp.float32
    )
    query_f = query_blk.astype(jnp.float32)
    carried = jnp.einsum("cthd,chde->cthe", query_f, states, precision=highest)
    attended = within + carried
    inv_rms = lax.rsqrt(jnp.mean(attended * attended, axis=-1, keepdims=True) + epsilon)
    unit_rows = attended * inv_rms
    normed_rows = (unit_rows * head_gain).astype(jnp.bfloat16).reshape(token_count, local_width)
    exchanged = lax.all_to_all(normed_rows, "head", split_axis=0, concat_axis=1, tiled=True)
    summed = jnp.dot(
        exchanged,
        lax.all_gather(w_out, "head", axis=0, tiled=True),
        preferred_element_type=jnp.float32,
    )
    layer_out = summed.astype(jnp.bfloat16)[None]
    grad_normed = jnp.einsum(
        "tm,fm->tf", cotangent[0], w_out, preferred_element_type=jnp.float32
    ).reshape(blocks)
    gain_part = jnp.sum(grad_normed * unit_rows, axis=(0, 1))
    total_tokens = seq_size * lax.axis_size("dp") * token_count
    gain_grad = lax.psum(gain_part, ("seq", "dp")) / math.sqrt(total_tokens)
    scaled = grad_normed * head_gain
    grad_attended = inv_rms * (
        scaled - unit_rows * jnp.mean(scaled * unit_rows, axis=-1, keepdims=True)
    )
    grad_bf = grad_attended.astype(jnp.bfloat16)
    query_term = jnp.einsum(
        "cthd,cthe->chde", query_blk, grad_bf, preferred_element_type=jnp.float32
    )
    first_pick = jnp.where(doc_float == doc_float[0], 1.0, 0.0).astype(jnp.float32)
    own_grad = jnp.einsum("c,chde->hde", first_pick, query_term, precision=highest)
    incoming_grad, grad_doc = double_chain((own_grad, doc_float), move_backward, seq_size)
    take_back = jnp.where(doc_float == grad_doc[0], 1.0, 0.0).astype(jnp.float32)
    grad_states = (
        jnp.einsum("cj,jhde->chde", after_mask, query_term, precision=highest)
        + take_back[:, None, None, None] * incoming_grad
    )
    grad_scores = jnp.einsum(
        "cthe,cshe->chts", grad_bf, value_blk, preferred_element_type=jnp.float32
    )
    grad_weights = jnp.where(causal, grad_scores, 0.0).astype(jnp.bfloat16)
    grad_f = grad_bf.astype(jnp.float32)
    query_grad = jnp.einsum(
        "chts,cshd->cthd", grad_weights, key_blk, preferred_element_type=jnp.float32
    ) + jnp.einsum("cthe,chde->cthd", grad_f, states, precision=highest)
    key_grad = jnp.einsum(
        "chts,cthd->cshd", grad_weights, query_blk, preferred_element_type=jnp.float32
    ) + jnp.einsum("cshe,chde->cshd", value_blk.astype(jnp.float32), grad_states, precision=highest)
    value_grad = jnp.einsum(
        "chts,cthe->cshe", attn_weights, grad_bf, preferred_element_type=jnp.float32
    ) + jnp.einsum("cshd,chde->cshe", key_blk.astype(jnp.float32), grad_states, precision=highest)
    out_shape = (1, token_count, local_width)
    return (
        layer_out,
        query_grad.astype(jnp.bfloat16).reshape(out_shape),
        key_grad.astype(jnp.bfloat16).reshape(out_shape),
        value_grad.astype(jnp.bfloat16).reshape(out_shape),
        gain_grad,
    )


def solution(mesh):
    return jax.shard_map(
        on_device,
        mesh=mesh,
        in_specs=(
            P("dp", "seq", "head"),
            P("dp", "seq", "head"),
            P("dp", "seq", "head"),
            P("dp", "seq"),
            P("head", None),
            P("head", None),
            P("dp", "seq", None),
        ),
        out_specs=(
            P("dp", ("seq", "head"), None),
            P("dp", "seq", "head"),
            P("dp", "seq", "head"),
            P("dp", "seq", "head"),
            P("head", None),
        ),
        check_vma=False,
    )
```

profile of v0, /device:TPU:7, one launch (start us, length us, event | category | flops | bytes accessed | tf_op | source)
XLA Modules:
  0.0 170.7 jit_solution(11719621536188737796)
XLA Ops:
  7.2 0.0 copy-start
  7.2 0.0 all-gather.2.cloned.1.call-start
  8.0 1.0 reshape.195
  9.0 0.2 copy.35
  9.2 1.0 reshape.196
  10.2 0.2 broadcast_multiply_fusion
  10.5 3.2 %collective-permute-start.4 = (f32[4,128,128]{2,1,0:T(8,128)S(1)}, f32[4,128,128]{2,1,0:T(8,128)S(1)}, u32[]{:S(2)}, u32[]{:S(2)}) collective-permute-start(f32[4,128,128]{2,1,0:T(8,128)S(1)} %get-tuple-element.19), channel_id=1, source_target_pairs={{0,4},{4,8},{8,12},{12,16},{16,20},{20,24},{24,28},{1,5},{5,9},{9,... | collective-permute-start | bytes 786440 | tf_op jit(solution)/shard_map/ppermute | solution.py:14
  13.6 5.9 %collective-permute-done.4 = f32[4,128,128]{2,1,0:T(8,128)S(1)} collective-permute-done((f32[4,128,128]{2,1,0:T(8,128)S(1)}, f32[4,128,128]{2,1,0:T(8,128)S(1)}, u32[]{:S(2)}, u32[]{:S(2)}) %collective-permute-start.4) | collective-permute-done | bytes 262176 | tf_op jit(solution)/shard_map/ppermute | solution.py:14
  19.5 4.0 %collective-permute-start.5 = (f32[4,128,128]{2,1,0:T(8,128)S(1)}, f32[4,128,128]{2,1,0:T(8,128)S(1)}, u32[]{:S(2)}, u32[]{:S(2)}) collective-permute-start(f32[4,128,128]{2,1,0:T(8,128)S(1)} %collective-permute-done.4), channel_id=1, source_target_pairs={{0,4},{4,8},{8,12},{12,16},{16,20},{20,24},{24,28},{1,5},{5,9},{9,... | collective-permute-start | bytes 786440 | tf_op jit(solution)/shard_map/ppermute | solution.py:14
  23.6 4.1 %collective-permute-start = (f32[1]{0:T(128)}, f32[1]{0:T(128)}, u32[]{:S(2)}, u32[]{:S(2)}) collective-permute-start(f32[1]{0:T(128)} %bitcast.1), channel_id=1, source_target_pairs={{0,4},{4,8},{8,12},{12,16},{16,20},{20,24},{24,28},{1,5},{5,9},{9,... | collective-permute-start | bytes 20 | tf_op jit(solution)/shard_map/ppermute | solution.py:14
  27.6 0.0 all-gather.2.cloned.1.call-update
  27.7 0.1 reshape.194
  27.8 0.4 collective-permute-done
  28.2 4.4 %collective-permute-start.1 = (f32[1]{0:T(128)}, f32[1]{0:T(128)}, u32[]{:S(2)}, u32[]{:S(2)}) collective-permute-start(f32[1]{0:T(128)} %collective-permute-done), channel_id=1, source_target_pairs={{0,4},{4,8},{8,12},{12,16},{16,20},{20,24},{24,28},{1,5},{5,9},{9,... | collective-permute-start | bytes 20 | tf_op jit(solution)/shard_map/ppermute | solution.py:14
  33.2 0.3 collective-permute-done.1
  34.8 0.0 collective-permute-done.5
  34.8 0.0 copy-start.3
  34.8 3.2 %collective-permute-start.6 = (f32[4,128,128]{2,1,0:T(8,128)S(1)}, f32[4,128,128]{2,1,0:T(8,128)S(1)}, u32[]{:S(2)}, u32[]{:S(2)}) collective-permute-start(f32[4,128,128]{2,1,0:T(8,128)S(1)} %fusion.14), channel_id=1, source_target_pairs={{0,8},{4,12},{8,16},{12,20},{16,24},{20,28},{1,9},{5,13},{9,17},{1... | collective-permute-start | bytes 786440 | tf_op jit(solution)/shard_map/ppermute | solution.py:14
  38.1 2.7 %fusion.7 = f32[256,512]{0,1:T(8,128)S(1)} fusion(bf16[512,2048]{1,0:T(8,128)(2,1)} %param.12, bf16[1,256,2048]{2,1,0:T(8,128)(2,1)S(1)} %copy-done), kind=kOutput, calls=%fused_computation.17 | convolution fusion | flops 536870912 | bytes 3670016 | tf_op jit(solution)/shard_map/tm,fm->tf/dot_general | solution.py:92
  42.0 3.9 %collective-permute-start.2 = (f32[1]{0:T(128)}, f32[1]{0:T(128)}, u32[]{:S(2)}, u32[]{:S(2)}) collective-permute-start(f32[1]{0:T(128)} %select_n.117), channel_id=1, source_target_pairs={{0,8},{4,12},{8,16},{12,20},{16,24},{20,28},{1,9},{5,13},{9,17},{1... | collective-permute-start | bytes 20 | tf_op jit(solution)/shard_map/ppermute | solution.py:14
  46.6 4.2 %collective-permute-start.7 = (f32[4,128,128]{2,1,0:T(8,128)S(1)}, f32[4,128,128]{2,1,0:T(8,128)S(1)}, u32[]{:S(2)}, u32[]{:S(2)}) collective-permute-start(f32[4,128,128]{2,1,0:T(8,128)S(1)} %fusion.13), channel_id=1, source_target_pairs={{0,16},{4,20},{8,24},{12,28},{1,17},{5,21},{9,25},{13,29},{2,18},{... | collective-permute-start | bytes 786440 | tf_op jit(solution)/shard_map/ppermute | solution.py:14
  50.8 0.3 fusion.1
  51.1 0.3 convolution_bitcast_fusion.2
  52.1 2.1 %collective-permute-start.3 = (f32[1]{0:T(128)}, f32[1]{0:T(128)}, u32[]{:S(2)}, u32[]{:S(2)}) collective-permute-start(f32[1]{0:T(128)} %select_n.118), channel_id=1, source_target_pairs={{0,16},{4,20},{8,24},{12,28},{1,17},{5,21},{9,25},{13,29},{2,18},{... | collective-permute-start | bytes 20 | tf_op jit(solution)/shard_map/ppermute | solution.py:14
  55.5 0.1 fusion.16
  55.5 0.5 multiply_reduce_fusion.2
  56.0 0.2 multiply_reduce_fusion
  56.3 0.9 fusion.19
  57.1 0.2 fusion.28
  57.4 4.2 %collective-permute-start.12 = (f32[4,128,128]{1,2,0:T(8,128)S(1)}, f32[4,128,128]{1,2,0:T(8,128)S(1)}, u32[]{:S(2)}, u32[]{:S(2)}) collective-permute-start(f32[4,128,128]{1,2,0:T(8,128)S(1)} %multiply_bitcast_fusion), channel_id=1, source_target_pairs={{4,0},{8,4},{12,8},{16,12},{20,16},{24,20},{28,24},{5,1},{9,5},{13... | collective-permute-start | bytes 786440 | tf_op jit(solution)/shard_map/ppermute | solution.py:14
  61.5 3.3 %collective-permute-start.8 = (f32[1]{0:T(128)}, f32[1]{0:T(128)}, u32[]{:S(2)}, u32[]{:S(2)}) collective-permute-start(f32[1]{0:T(128)} %bitcast.1), channel_id=1, source_target_pairs={{4,0},{8,4},{12,8},{16,12},{20,16},{24,20},{28,24},{5,1},{9,5},{13... | collective-permute-start | bytes 20 | tf_op jit(solution)/shard_map/ppermute | solution.py:14
  64.9 7.3 %collective-permute-done.8 = f32[1]{0:T(128)} collective-permute-done((f32[1]{0:T(128)}, f32[1]{0:T(128)}, u32[]{:S(2)}, u32[]{:S(2)}) %collective-permute-start.8) | collective-permute-done | bytes 36 | tf_op jit(solution)/shard_map/ppermute | solution.py:14
  72.1 1.9 %collective-permute-start.9 = (f32[1]{0:T(128)}, f32[1]{0:T(128)}, u32[]{:S(2)}, u32[]{:S(2)}) collective-permute-start(f32[1]{0:T(128)} %collective-permute-done.8), channel_id=1, source_target_pairs={{4,0},{8,4},{12,8},{16,12},{20,16},{24,20},{28,24},{5,1},{9,5},{13... | collective-permute-start | bytes 20 | tf_op jit(solution)/shard_map/ppermute | solution.py:14
  74.6 2.8 %collective-permute-done.9 = f32[1]{0:T(128)} collective-permute-done((f32[1]{0:T(128)}, f32[1]{0:T(128)}, u32[]{:S(2)}, u32[]{:S(2)}) %collective-permute-start.9) | collective-permute-done | bytes 36 | tf_op jit(solution)/shard_map/ppermute | solution.py:14
  78.7 1.3 collective-permute-start.10
  81.2 2.3 %collective-permute-done.10 = f32[1]{0:T(128)} collective-permute-done((f32[1]{0:T(128)}, f32[1]{0:T(128)}, u32[]{:S(2)}, u32[]{:S(2)}) %collective-permute-start.10) | collective-permute-done | bytes 36 | tf_op jit(solution)/shard_map/ppermute | solution.py:14
  84.1 1.3 collective-permute-start.11
  86.1 3.4 %collective-permute-done.11 = f32[1]{0:T(128)} collective-permute-done((f32[1]{0:T(128)}, f32[1]{0:T(128)}, u32[]{:S(2)}, u32[]{:S(2)}) %collective-permute-start.11) | collective-permute-done | bytes 36 | tf_op jit(solution)/shard_map/ppermute | solution.py:14
  90.8 1.9 %collective-permute-start.13 = (f32[4,128,128]{1,2,0:T(8,128)S(1)}, f32[4,128,128]{1,2,0:T(8,128)S(1)}, u32[]{:S(2)}, u32[]{:S(2)}) collective-permute-start(f32[4,128,128]{1,2,0:T(8,128)S(1)} %collective-permute-done.12), channel_id=1, source_target_pairs={{4,0},{8,4},{12,8},{16,12},{20,16},{24,20},{28,24},{5,1},{9,5},{13... | collective-permute-start | bytes 786440 | tf_op jit(solution)/shard_map/ppermute | solution.py:14
  92.7 0.3 fusion.2
  93.1 0.0 copy-start.1
  93.1 0.3 convolution_bitcast_fusion.1
  93.4 5.4 %collective-permute-done.13 = f32[4,128,128]{1,2,0:T(8,128)S(1)} collective-permute-done((f32[4,128,128]{1,2,0:T(8,128)S(1)}, f32[4,128,128]{1,2,0:T(8,128)S(1)}, u32[]{:S(2)}, u32[]{:S(2)}) %collective-permute-start.13) | collective-permute-done | bytes 262176 | tf_op jit(solution)/shard_map/ppermute | solution.py:14
  98.9 1.3 collective-permute-start.14
  100.2 0.4 fusion.4
  100.5 0.8 copy.50
  101.4 1.0 all_to_all.14
  102.4 0.7 copy.39
  103.1 3.4 %all-to-all-start = ((bf16[2,128,512]{1,2,0:T(8,128)(2,1)}), bf16[2,128,512]{1,2,0:T(8,128)(2,1)S(1)}, u32[]{:S(2)}, u32[]{:S(2)}) async-start(bf16[2,128,512]{1,2,0:T(8,128)(2,1)} %copy.39), calls=%async_computation | async-start | bytes 524288 | tf_op jit(solution)/shard_map/all_to_all | solution.py:85
  106.6 33.1 %psum.7 = f32[4,128]{1,0:T(4,128)S(1)} all-reduce(f32[4,128]{1,0:T(4,128)S(1)} %get-tuple-element.15), channel_id=1, replica_groups=mesh['seq'=8,'head'=2,'dp'=2] {'seq','dp'}, use_global_device_ids=true, to_apply=%region_3.4 | all-reduce | flops 512 | bytes 4096 | tf_op jit(solution)/shard_map/psum | solution.py:97
  139.7 0.2 fusion.32
  139.9 0.0 collective-permute-done.14
  140.0 1.0 fusion.10
  140.9 1.3 collective-permute-start.15
  142.2 0.6 broadcast_multiply_fusion.2
  142.8 1.3 convolution_bitcast_fusion
  144.1 13.4 %collective-permute-done.15 = f32[4,128,128]{1,2,0:T(8,128)S(1)} collective-permute-done((f32[4,128,128]{1,2,0:T(8,128)S(1)}, f32[4,128,128]{1,2,0:T(8,128)S(1)}, u32[]{:S(2)}, u32[]{:S(2)}) %collective-permute-start.15) | collective-permute-done | bytes 262176 | tf_op jit(solution)/shard_map/ppermute | solution.py:14
  157.6 0.1 fusion.18
  157.6 0.4 fusion.6
  158.0 0.8 copy.52
  158.9 0.4 fusion.5
  159.3 0.8 copy.51
  160.2 0.0 all-to-all-done
  160.2 3.7 %fusion = bf16[1,128,2048]{2,1,0:T(8,128)(2,1)} fusion(bf16[128,1024]{0,1:T(8,128)(2,1)S(1)} %bitcast.79, bf16[1024,2048]{1,0:T(8,128)(2,1)} %all-gather.2.cloned.1.call-done), kind=kOutput, calls=%fused_computation.1 | convolution fusion | flops 537133056 | bytes 4980736 | tf_op jit(solution)/shard_map/dot_general | solution.py:86
  (18 shorter events, 0.2 us)
Async XLA Ops:
  7.2 30.9 %copy-start = (bf16[1,256,2048]{2,1,0:T(8,128)(2,1)S(1)}, bf16[1,256,2048]{2,1,0:T(8,128)(2,1)}, u32[]{:S(2)}) copy-start(bf16[1,256,2048]{2,1,0:T(8,128)(2,1)} %param.13) | copy-start | bytes 3145732
  7.2 20.5 %copy-start.2 = (bf16[1,256,512]{2,1,0:T(8,128)(2,1)S(1)}, bf16[1,256,512]{2,1,0:T(8,128)(2,1)}, u32[]{:S(2)}) copy-start(bf16[1,256,512]{2,1,0:T(8,128)(2,1)} %param.7) | copy-start | bytes 786436
  7.2 153.0 %all-gather.2.cloned.1.call-start = ((), (), s32[]{:S(2)}) async-start(), calls=%async_computation.1 | async-start | bytes 6291456 | tf_op jit(solution)/shard_map/all_gather | solution.py:88
  10.5 9.1 %collective-permute-start.4 = (f32[4,128,128]{2,1,0:T(8,128)S(1)}, f32[4,128,128]{2,1,0:T(8,128)S(1)}, u32[]{:S(2)}, u32[]{:S(2)}) collective-permute-start(f32[4,128,128]{2,1,0:T(8,128)S(1)} %get-tuple-element.19), channel_id=1, source_target_pairs={{0,4},{4,8},{8,12},{12,16},{16,20},{20,24},{24,28},{1,5},{5,9},{9,... | collective-permute-start | bytes 786440 | tf_op jit(solution)/shard_map/ppermute | solution.py:14
  19.5 15.3 %collective-permute-start.5 = (f32[4,128,128]{2,1,0:T(8,128)S(1)}, f32[4,128,128]{2,1,0:T(8,128)S(1)}, u32[]{:S(2)}, u32[]{:S(2)}) collective-permute-start(f32[4,128,128]{2,1,0:T(8,128)S(1)} %collective-permute-done.4), channel_id=1, source_target_pairs={{0,4},{4,8},{8,12},{12,16},{16,20},{20,24},{24,28},{1,5},{5,9},{9,... | collective-permute-start | bytes 786440 | tf_op jit(solution)/shard_map/ppermute | solution.py:14
  23.6 4.6 %collective-permute-start = (f32[1]{0:T(128)}, f32[1]{0:T(128)}, u32[]{:S(2)}, u32[]{:S(2)}) collective-permute-start(f32[1]{0:T(128)} %bitcast.1), channel_id=1, source_target_pairs={{0,4},{4,8},{8,12},{12,16},{16,20},{20,24},{24,28},{1,5},{5,9},{9,... | collective-permute-start | bytes 20 | tf_op jit(solution)/shard_map/ppermute | solution.py:14
  28.2 5.3 %collective-permute-start.1 = (f32[1]{0:T(128)}, f32[1]{0:T(128)}, u32[]{:S(2)}, u32[]{:S(2)}) collective-permute-start(f32[1]{0:T(128)} %collective-permute-done), channel_id=1, source_target_pairs={{0,4},{4,8},{8,12},{12,16},{16,20},{20,24},{24,28},{1,5},{5,9},{9,... | collective-permute-start | bytes 20 | tf_op jit(solution)/shard_map/ppermute | solution.py:14
  34.8 21.2 %copy-start.3 = (f32[4,128]{1,0:T(4,128)S(1)}, f32[4,128]{1,0:T(4,128)}, u32[]{:S(2)}) copy-start(f32[4,128]{1,0:T(4,128)} %param.11) | copy-start | bytes 6148
  34.8 11.7 %collective-permute-start.6 = (f32[4,128,128]{2,1,0:T(8,128)S(1)}, f32[4,128,128]{2,1,0:T(8,128)S(1)}, u32[]{:S(2)}, u32[]{:S(2)}) collective-permute-start(f32[4,128,128]{2,1,0:T(8,128)S(1)} %fusion.14), channel_id=1, source_target_pairs={{0,8},{4,12},{8,16},{12,20},{16,24},{20,28},{1,9},{5,13},{9,17},{1... | collective-permute-start | bytes 786440 | tf_op jit(solution)/shard_map/ppermute | solution.py:14
  42.0 3.9 %collective-permute-start.2 = (f32[1]{0:T(128)}, f32[1]{0:T(128)}, u32[]{:S(2)}, u32[]{:S(2)}) collective-permute-start(f32[1]{0:T(128)} %select_n.117), channel_id=1, source_target_pairs={{0,8},{4,12},{8,16},{12,20},{16,24},{20,28},{1,9},{5,13},{9,17},{1... | collective-permute-start | bytes 20 | tf_op jit(solution)/shard_map/ppermute | solution.py:14
  46.6 8.8 %collective-permute-start.7 = (f32[4,128,128]{2,1,0:T(8,128)S(1)}, f32[4,128,128]{2,1,0:T(8,128)S(1)}, u32[]{:S(2)}, u32[]{:S(2)}) collective-permute-start(f32[4,128,128]{2,1,0:T(8,128)S(1)} %fusion.13), channel_id=1, source_target_pairs={{0,16},{4,20},{8,24},{12,28},{1,17},{5,21},{9,25},{13,29},{2,18},{... | collective-permute-start | bytes 786440 | tf_op jit(solution)/shard_map/ppermute | solution.py:14
  52.1 2.1 %collective-permute-start.3 = (f32[1]{0:T(128)}, f32[1]{0:T(128)}, u32[]{:S(2)}, u32[]{:S(2)}) collective-permute-start(f32[1]{0:T(128)} %select_n.118), channel_id=1, source_target_pairs={{0,16},{4,20},{8,24},{12,28},{1,17},{5,21},{9,25},{13,29},{2,18},{... | collective-permute-start | bytes 20 | tf_op jit(solution)/shard_map/ppermute | solution.py:14
  57.4 33.4 %collective-permute-start.12 = (f32[4,128,128]{1,2,0:T(8,128)S(1)}, f32[4,128,128]{1,2,0:T(8,128)S(1)}, u32[]{:S(2)}, u32[]{:S(2)}) collective-permute-start(f32[4,128,128]{1,2,0:T(8,128)S(1)} %multiply_bitcast_fusion), channel_id=1, source_target_pairs={{4,0},{8,4},{12,8},{16,12},{20,16},{24,20},{28,24},{5,1},{9,5},{13... | collective-permute-start | bytes 786440 | tf_op jit(solution)/shard_map/ppermute | solution.py:14
  61.5 10.6 %collective-permute-start.8 = (f32[1]{0:T(128)}, f32[1]{0:T(128)}, u32[]{:S(2)}, u32[]{:S(2)}) collective-permute-start(f32[1]{0:T(128)} %bitcast.1), channel_id=1, source_target_pairs={{4,0},{8,4},{12,8},{16,12},{20,16},{24,20},{28,24},{5,1},{9,5},{13... | collective-permute-start | bytes 20 | tf_op jit(solution)/shard_map/ppermute | solution.py:14
  72.1 5.3 %collective-permute-start.9 = (f32[1]{0:T(128)}, f32[1]{0:T(128)}, u32[]{:S(2)}, u32[]{:S(2)}) collective-permute-start(f32[1]{0:T(128)} %collective-permute-done.8), channel_id=1, source_target_pairs={{4,0},{8,4},{12,8},{16,12},{20,16},{24,20},{28,24},{5,1},{9,5},{13... | collective-permute-start | bytes 20 | tf_op jit(solution)/shard_map/ppermute | solution.py:14
  78.7 4.8 %collective-permute-start.10 = (f32[1]{0:T(128)}, f32[1]{0:T(128)}, u32[]{:S(2)}, u32[]{:S(2)}) collective-permute-start(f32[1]{0:T(128)} %select_n.135), channel_id=1, source_target_pairs={{8,0},{12,4},{16,8},{20,12},{24,16},{28,20},{9,1},{13,5},{17,9},{2... | collective-permute-start | bytes 20 | tf_op jit(solution)/shard_map/ppermute | solution.py:14
  84.1 5.4 %collective-permute-start.11 = (f32[1]{0:T(128)}, f32[1]{0:T(128)}, u32[]{:S(2)}, u32[]{:S(2)}) collective-permute-start(f32[1]{0:T(128)} %select_n.136), channel_id=1, source_target_pairs={{16,0},{20,4},{24,8},{28,12},{17,1},{21,5},{25,9},{29,13},{18,2},{... | collective-permute-start | bytes 20 | tf_op jit(solution)/shard_map/ppermute | solution.py:14
  90.8 8.0 %collective-permute-start.13 = (f32[4,128,128]{1,2,0:T(8,128)S(1)}, f32[4,128,128]{1,2,0:T(8,128)S(1)}, u32[]{:S(2)}, u32[]{:S(2)}) collective-permute-start(f32[4,128,128]{1,2,0:T(8,128)S(1)} %collective-permute-done.12), channel_id=1, source_target_pairs={{4,0},{8,4},{12,8},{16,12},{20,16},{24,20},{28,24},{5,1},{9,5},{13... | collective-permute-start | bytes 786440 | tf_op jit(solution)/shard_map/ppermute | solution.py:14
  93.1 7.4 %copy-start.1 = (bf16[4,256,256]{2,1,0:T(8,128)(2,1)}, bf16[4,256,256]{2,1,0:T(8,128)(2,1)S(1)}, u32[]{:S(2)}) copy-start(bf16[4,256,256]{2,1,0:T(8,128)(2,1)S(1)} %fusion.2) | copy-start | bytes 1572868
  98.9 41.1 %collective-permute-start.14 = (f32[4,128,128]{1,2,0:T(8,128)S(1)}, f32[4,128,128]{1,2,0:T(8,128)}, u32[]{:S(2)}, u32[]{:S(2)}) collective-permute-start(f32[4,128,128]{1,2,0:T(8,128)S(1)} %fusion.11), channel_id=1, source_target_pairs={{8,0},{12,4},{16,8},{20,12},{24,16},{28,20},{9,1},{13,5},{17,9},{2... | collective-permute-start | bytes 786440 | tf_op jit(solution)/shard_map/ppermute | solution.py:14
  103.1 57.0 %all-to-all-start = ((bf16[2,128,512]{1,2,0:T(8,128)(2,1)}), bf16[2,128,512]{1,2,0:T(8,128)(2,1)S(1)}, u32[]{:S(2)}, u32[]{:S(2)}) async-start(bf16[2,128,512]{1,2,0:T(8,128)(2,1)} %copy.39), calls=%async_computation | async-start | bytes 524288 | tf_op jit(solution)/shard_map/all_to_all | solution.py:85
  140.9 16.6 %collective-permute-start.15 = (f32[4,128,128]{1,2,0:T(8,128)S(1)}, f32[4,128,128]{1,2,0:T(8,128)S(1)}, u32[]{:S(2)}, u32[]{:S(2)}) collective-permute-start(f32[4,128,128]{1,2,0:T(8,128)S(1)} %fusion.10), channel_id=1, source_target_pairs={{16,0},{20,4},{24,8},{28,12},{17,1},{21,5},{25,9},{29,13},{18,2},{... | collective-permute-start | bytes 786440 | tf_op jit(solution)/shard_map/ppermute | solution.py:14
Sparse Core Ops, SparseCore 0:
  27.8 57.8 all-gather.1
where the time goes:
time: 172 us; the launch traced here: 171 us
  starting transfers between devices  49.1 us (29%)
  waiting for transfers between devices  41.2 us (24%)
  blocking collectives  33.1 us (19%)
  between operations  26.5 us (15%)
  matrix products  11.2 us (7%)
  local copies, waits for them, and re-layouts  6.59 us (4%)
  other arithmetic  2.95 us (2%)
    ppermute x16, starting transfers between devices, shifted(): return lax.ppermute(block, axis, route)  45.6 us
    ppermute x16, waiting for transfers between devices, shifted(): return lax.ppermute(block, axis, route)  41.2 us
    psum x1, blocking collectives, on_device(): gain_grad = lax.psum(gain_part, ('seq', 'dp')) / math.sqrt(total_tokens)  33.1 us
    dot_general x1, matrix products, on_device(): jnp.dot(exchanged, lax.all_gather(w_out, 'head', axis=0, tiled=True), pre...  3.72 us
  transfers between devices with their start and end apart: 18, of which 9 were waited for; matrix products, arithmetic and copies ran while one was open for 8% of the time, Pallas kernels for 0%

commit v1 on v0

--- a/solution.py
+++ b/solution.py
@@ -82,7 +82,10 @@
     inv_rms = lax.rsqrt(jnp.mean(attended * attended, axis=-1, keepdims=True) + epsilon)
     unit_rows = attended * inv_rms
     normed_rows = (unit_rows * head_gain).astype(jnp.bfloat16).reshape(token_count, local_width)
-    exchanged = lax.all_to_all(normed_rows, "head", split_axis=0, concat_axis=1, tiled=True)
+    size = lax.axis_size("head")
+    tiles = jnp.stack(jnp.split(normed_rows, size, axis=0), axis=0)
+    tiles = lax.all_to_all(tiles, "head", split_axis=0, concat_axis=0)
+    exchanged = jnp.concatenate(tiles, axis=1)
     summed = jnp.dot(
         exchanged,
         lax.all_gather(w_out, "head", axis=0, tiled=True),

time: 172 us -> 170 us (0.988)
  waiting for transfers between devices: 41.2 us -> 31.2 us
  starting transfers between devices: 49.1 us -> 55 us
  blocking collectives: 33.1 us -> 36.9 us
    ppermute x16, waiting for transfers between devices: 41.2 us -> 31.1 us  [shifted(): return lax.ppermute(block, axis, route)]
    ppermute x16, starting transfers between devices: 45.6 us -> 51.4 us  [shifted(): return lax.ppermute(block, axis, route)]
    psum x1, blocking collectives: 33.1 us -> 36.9 us  [on_device(): gain_grad = lax.psum(gain_part, ('seq', 'dp')) / math.sqrt(total_tokens)]
    all_to_all x2 -> x0, local copies, waits for them, and re-layouts: 1.76 us -> none  [on_device(): lax.all_to_all(normed_rows, 'head', split_axis=0, concat_axis=1, tiled=True)]
  transfers between devices with their start and end apart: 18 -> 18, of which waited for: 9 -> 7; matrix products, arithmetic and copies ran while one was open for 8% -> 8% of each run, Pallas kernels for 0% -> 0%
where the time goes in v1:
time: 170 us; the launch traced here: 169 us
  starting transfers between devices  55 us (32%)
  blocking collectives  36.9 us (22%)
  waiting for transfers between devices  31.2 us (18%)
  between operations  26.8 us (16%)
  matrix products  11.2 us (7%)
  local copies, waits for them, and re-layouts  4.88 us (3%)
  other arithmetic  2.98 us (2%)
    ppermute x16, starting transfers between devices, shifted(): return lax.ppermute(block, axis, route)  51.4 us
    psum x1, blocking collectives, on_device(): gain_grad = lax.psum(gain_part, ('seq', 'dp')) / math.sqrt(total_tokens)  36.9 us
    ppermute x16, waiting for transfers between devices, shifted(): return lax.ppermute(block, axis, route)  31.1 us
    dot_general x1, matrix products, on_device(): jnp.dot(exchanged, lax.all_gather(w_out, 'head', axis=0, tiled=True), pre...  3.72 us
    all_to_all x1, starting transfers between devices, on_device(): tiles = lax.all_to_all(tiles, 'head', split_axis=0, concat_axis=0)  3.56 us
  transfers between devices with their start and end apart: 18, of which 7 were waited for; matrix products, arithmetic and copies ran while one was open for 8% of the time, Pallas kernels for 0%

profile of v1, /device:TPU:7, one launch (start us, length us, event | category | flops | bytes accessed | tf_op | source)
XLA Modules:
  0.0 168.9 jit_solution(3950437468865324996)
XLA Ops:
  7.2 0.0 copy-start
  7.2 0.0 copy-start.2
  7.2 0.0 all-gather.2.cloned.1.call-start
  8.0 1.0 reshape.201
  9.0 0.2 copy.15
  9.2 1.0 reshape.202
  10.2 0.2 broadcast_multiply_fusion
  10.5 3.2 %collective-permute-start.4 = (f32[4,128,128]{2,1,0:T(8,128)S(1)}, f32[4,128,128]{2,1,0:T(8,128)S(1)}, u32[]{:S(2)}, u32[]{:S(2)}) collective-permute-start(f32[4,128,128]{2,1,0:T(8,128)S(1)} %get-tuple-element.16), channel_id=1, source_target_pairs={{0,4},{4,8},{8,12},{12,16},{16,20},{20,24},{24,28},{1,5},{5,9},{9,... | collective-permute-start | bytes 786440 | tf_op jit(solution)/shard_map/ppermute | solution.py:14
  13.6 5.9 %collective-permute-done.4 = f32[4,128,128]{2,1,0:T(8,128)S(1)} collective-permute-done((f32[4,128,128]{2,1,0:T(8,128)S(1)}, f32[4,128,128]{2,1,0:T(8,128)S(1)}, u32[]{:S(2)}, u32[]{:S(2)}) %collective-permute-start.4) | collective-permute-done | bytes 262176 | tf_op jit(solution)/shard_map/ppermute | solution.py:14
  19.5 4.0 %collective-permute-start.5 = (f32[4,128,128]{2,1,0:T(8,128)S(1)}, f32[4,128,128]{2,1,0:T(8,128)S(1)}, u32[]{:S(2)}, u32[]{:S(2)}) collective-permute-start(f32[4,128,128]{2,1,0:T(8,128)S(1)} %collective-permute-done.4), channel_id=1, source_target_pairs={{0,4},{4,8},{8,12},{12,16},{16,20},{20,24},{24,28},{1,5},{5,9},{9,... | collective-permute-start | bytes 786440 | tf_op jit(solution)/shard_map/ppermute | solution.py:14
  23.6 4.1 %collective-permute-start = (f32[1]{0:T(128)}, f32[1]{0:T(128)}, u32[]{:S(2)}, u32[]{:S(2)}) collective-permute-start(f32[1]{0:T(128)} %bitcast.1), channel_id=1, source_target_pairs={{0,4},{4,8},{8,12},{12,16},{16,20},{20,24},{24,28},{1,5},{5,9},{9,... | collective-permute-start | bytes 20 | tf_op jit(solution)/shard_map/ppermute | solution.py:14
  27.6 2.6 %collective-permute-start.8 = (f32[1]{0:T(128)}, f32[1]{0:T(128)}, u32[]{:S(2)}, u32[]{:S(2)}) collective-permute-start(f32[1]{0:T(128)} %bitcast.1), channel_id=1, source_target_pairs={{4,0},{8,4},{12,8},{16,12},{20,16},{24,20},{28,24},{5,1},{9,5},{13... | collective-permute-start | bytes 20 | tf_op jit(solution)/shard_map/ppermute | solution.py:14
  30.3 0.0 all-gather.2.cloned.1.call-update
  30.3 0.1 reshape.200
  30.4 4.3 %collective-permute-start.1 = (f32[1]{0:T(128)}, f32[1]{0:T(128)}, u32[]{:S(2)}, u32[]{:S(2)}) collective-permute-start(f32[1]{0:T(128)} %collective-permute-done), channel_id=1, source_target_pairs={{0,4},{4,8},{8,12},{12,16},{16,20},{20,24},{24,28},{1,5},{5,9},{9,... | collective-permute-start | bytes 20 | tf_op jit(solution)/shard_map/ppermute | solution.py:14
  35.3 0.1 collective-permute-done.1
  36.7 0.0 collective-permute-done.5
  36.8 0.0 copy-start.3
  36.8 3.2 %collective-permute-start.6 = (f32[4,128,128]{2,1,0:T(8,128)S(1)}, f32[4,128,128]{2,1,0:T(8,128)S(1)}, u32[]{:S(2)}, u32[]{:S(2)}) collective-permute-start(f32[4,128,128]{2,1,0:T(8,128)S(1)} %fusion.14), channel_id=1, source_target_pairs={{0,8},{4,12},{8,16},{12,20},{16,24},{20,28},{1,9},{5,13},{9,17},{1... | collective-permute-start | bytes 786440 | tf_op jit(solution)/shard_map/ppermute | solution.py:14
  40.0 2.6 %fusion.7 = f32[256,512]{0,1:T(8,128)S(1)} fusion(bf16[512,2048]{1,0:T(8,128)(2,1)} %param.12, bf16[1,256,2048]{2,1,0:T(8,128)(2,1)S(1)} %copy-done), kind=kOutput, calls=%fused_computation.17 | convolution fusion | flops 536870912 | bytes 3670016 | tf_op jit(solution)/shard_map/tm,fm->tf/dot_general | solution.py:95
  43.9 3.9 %collective-permute-start.2 = (f32[1]{0:T(128)}, f32[1]{0:T(128)}, u32[]{:S(2)}, u32[]{:S(2)}) collective-permute-start(f32[1]{0:T(128)} %select_n.117), channel_id=1, source_target_pairs={{0,8},{4,12},{8,16},{12,20},{16,24},{20,28},{1,9},{5,13},{9,17},{1... | collective-permute-start | bytes 20 | tf_op jit(solution)/shard_map/ppermute | solution.py:14
  48.4 0.0 collective-permute-done.6
  48.4 3.9 %collective-permute-start.7 = (f32[4,128,128]{2,1,0:T(8,128)S(1)}, f32[4,128,128]{2,1,0:T(8,128)S(1)}, u32[]{:S(2)}, u32[]{:S(2)}) collective-permute-start(f32[4,128,128]{2,1,0:T(8,128)S(1)} %fusion.13), channel_id=1, source_target_pairs={{0,16},{4,20},{8,24},{12,28},{1,17},{5,21},{9,25},{13,29},{2,18},{... | collective-permute-start | bytes 786440 | tf_op jit(solution)/shard_map/ppermute | solution.py:14
  52.3 0.3 fusion.1
  52.6 0.3 convolution_bitcast_fusion.2
  53.0 4.6 %collective-permute-start.9 = (f32[1]{0:T(128)}, f32[1]{0:T(128)}, u32[]{:S(2)}, u32[]{:S(2)}) collective-permute-start(f32[1]{0:T(128)} %collective-permute-done.8), channel_id=1, source_target_pairs={{4,0},{8,4},{12,8},{16,12},{20,16},{24,20},{28,24},{5,1},{9,5},{13... | collective-permute-start | bytes 20 | tf_op jit(solution)/shard_map/ppermute | solution.py:14
  58.2 0.3 collective-permute-done.9
  59.8 1.3 collective-permute-start.10
  62.9 5.1 %collective-permute-start.3 = (f32[1]{0:T(128)}, f32[1]{0:T(128)}, u32[]{:S(2)}, u32[]{:S(2)}) collective-permute-start(f32[1]{0:T(128)} %select_n.118), channel_id=1, source_target_pairs={{0,16},{4,20},{8,24},{12,28},{1,17},{5,21},{9,25},{13,29},{2,18},{... | collective-permute-start | bytes 20 | tf_op jit(solution)/shard_map/ppermute | solution.py:14
  68.8 1.3 collective-permute-start.11
  71.4 2.6 %collective-permute-done.11 = f32[1]{0:T(128)} collective-permute-done((f32[1]{0:T(128)}, f32[1]{0:T(128)}, u32[]{:S(2)}, u32[]{:S(2)}) %collective-permute-start.11) | collective-permute-done | bytes 36 | tf_op jit(solution)/shard_map/ppermute | solution.py:14
  76.0 0.0 collective-permute-done.7
  76.1 0.1 fusion.16
  76.1 0.5 multiply_reduce_fusion.2
  76.6 0.2 multiply_reduce_fusion
  76.8 0.2 fusion.19
  77.0 0.2 fusion.28
  77.3 3.9 %collective-permute-start.12 = (f32[4,128,128]{1,2,0:T(8,128)S(1)}, f32[4,128,128]{1,2,0:T(8,128)S(1)}, u32[]{:S(2)}, u32[]{:S(2)}) collective-permute-start(f32[4,128,128]{1,2,0:T(8,128)S(1)} %multiply_bitcast_fusion), channel_id=1, source_target_pairs={{4,0},{8,4},{12,8},{16,12},{20,16},{24,20},{28,24},{5,1},{9,5},{13... | collective-permute-start | bytes 786440 | tf_op jit(solution)/shard_map/ppermute | solution.py:14
  81.2 0.3 fusion.2
  81.6 0.0 copy-start.1
  81.6 0.3 convolution_bitcast_fusion.1
  81.9 3.4 %collective-permute-done.12 = f32[4,128,128]{1,2,0:T(8,128)S(1)} collective-permute-done((f32[4,128,128]{1,2,0:T(8,128)S(1)}, f32[4,128,128]{1,2,0:T(8,128)S(1)}, u32[]{:S(2)}, u32[]{:S(2)}) %collective-permute-start.12) | collective-permute-done | bytes 262176 | tf_op jit(solution)/shard_map/ppermute | solution.py:14
  85.3 3.4 %collective-permute-start.13 = (f32[4,128,128]{1,2,0:T(8,128)S(1)}, f32[4,128,128]{1,2,0:T(8,128)S(1)}, u32[]{:S(2)}, u32[]{:S(2)}) collective-permute-start(f32[4,128,128]{1,2,0:T(8,128)S(1)} %collective-permute-done.12), channel_id=1, source_target_pairs={{4,0},{8,4},{12,8},{16,12},{20,16},{24,20},{28,24},{5,1},{9,5},{13... | collective-permute-start | bytes 786440 | tf_op jit(solution)/shard_map/ppermute | solution.py:14
  88.8 0.4 fusion.4
  89.1 5.4 %collective-permute-done.13 = f32[4,128,128]{1,2,0:T(8,128)S(1)} collective-permute-done((f32[4,128,128]{1,2,0:T(8,128)S(1)}, f32[4,128,128]{1,2,0:T(8,128)S(1)}, u32[]{:S(2)}, u32[]{:S(2)}) %collective-permute-start.13) | collective-permute-done | bytes 262176 | tf_op jit(solution)/shard_map/ppermute | solution.py:14
  94.5 1.3 collective-permute-start.14
  95.8 0.7 pad_maximum_fusion
  96.6 0.8 copy.29
  97.4 3.6 %all-to-all-start = ((bf16[2,128,512]{1,2,0:T(8,128)(2,1)}), bf16[2,128,512]{1,2,0:T(8,128)(2,1)S(1)}, u32[]{:S(2)}, u32[]{:S(2)}) async-start(bf16[2,128,512]{1,2,0:T(8,128)(2,1)} %pad_maximum_fusion), calls=%async_computation | async-start | bytes 524288 | tf_op jit(solution)/shard_map/all_to_all | solution.py:87
  101.0 36.9 %psum.7 = f32[4,128]{1,0:T(4,128)S(1)} all-reduce(f32[4,128]{1,0:T(4,128)S(1)} %get-tuple-element.10), channel_id=1, replica_groups=mesh['seq'=8,'head'=2,'dp'=2] {'seq','dp'}, use_global_device_ids=true, to_apply=%region_3.4 | all-reduce | flops 512 | bytes 4096 | tf_op jit(solution)/shard_map/psum | solution.py:100
  137.8 0.2 fusion.33
  138.1 0.0 collective-permute-done.14
  138.1 1.0 fusion.10
  139.1 1.3 collective-permute-start.15
  140.4 0.6 broadcast_multiply_fusion.2
  141.0 1.3 convolution_bitcast_fusion
  142.3 13.4 %collective-permute-done.15 = f32[4,128,128]{1,2,0:T(8,128)S(1)} collective-permute-done((f32[4,128,128]{1,2,0:T(8,128)S(1)}, f32[4,128,128]{1,2,0:T(8,128)S(1)}, u32[]{:S(2)}, u32[]{:S(2)}) %collective-permute-start.15) | collective-permute-done | bytes 262176 | tf_op jit(solution)/shard_map/ppermute | solution.py:14
  155.7 0.1 fusion.18
  155.8 0.4 fusion.6
  156.2 0.8 copy.31
  157.0 0.4 fusion.5
  157.4 0.8 copy.30
  158.3 0.0 all-to-all-done
  158.3 3.7 %fusion = bf16[1,128,2048]{2,1,0:T(8,128)(2,1)} fusion(bf16[128,1024]{0,1:T(8,128)(2,1)S(1)} %bitcast.77, bf16[1024,2048]{1,0:T(8,128)(2,1)} %all-gather.2.cloned.1.call-done), kind=kOutput, calls=%fused_computation.1 | convolution fusion | flops 537133056 | bytes 4980736 | tf_op jit(solution)/shard_map/dot_general | solution.py:89
  (18 shorter events, 0.2 us)
Async XLA Ops:
  7.2 32.8 %copy-start = (bf16[1,256,2048]{2,1,0:T(8,128)(2,1)S(1)}, bf16[1,256,2048]{2,1,0:T(8,128)(2,1)}, u32[]{:S(2)}) copy-start(bf16[1,256,2048]{2,1,0:T(8,128)(2,1)} %param.13) | copy-start | bytes 3145732
  7.2 23.1 %copy-start.2 = (bf16[1,256,512]{2,1,0:T(8,128)(2,1)S(1)}, bf16[1,256,512]{2,1,0:T(8,128)(2,1)}, u32[]{:S(2)}) copy-start(bf16[1,256,512]{2,1,0:T(8,128)(2,1)} %param.7) | copy-start | bytes 786436
  7.2 151.1 %all-gather.2.cloned.1.call-start = ((), (), s32[]{:S(2)}) async-start(), calls=%async_computation.1 | async-start | bytes 6291456 | tf_op jit(solution)/shard_map/all_gather | solution.py:91
  10.5 9.1 %collective-permute-start.4 = (f32[4,128,128]{2,1,0:T(8,128)S(1)}, f32[4,128,128]{2,1,0:T(8,128)S(1)}, u32[]{:S(2)}, u32[]{:S(2)}) collective-permute-start(f32[4,128,128]{2,1,0:T(8,128)S(1)} %get-tuple-element.16), channel_id=1, source_target_pairs={{0,4},{4,8},{8,12},{12,16},{16,20},{20,24},{24,28},{1,5},{5,9},{9,... | collective-permute-start | bytes 786440 | tf_op jit(solution)/shard_map/ppermute | solution.py:14
  19.5 17.2 %collective-permute-start.5 = (f32[4,128,128]{2,1,0:T(8,128)S(1)}, f32[4,128,128]{2,1,0:T(8,128)S(1)}, u32[]{:S(2)}, u32[]{:S(2)}) collective-permute-start(f32[4,128,128]{2,1,0:T(8,128)S(1)} %collective-permute-done.4), channel_id=1, source_target_pairs={{0,4},{4,8},{8,12},{12,16},{16,20},{20,24},{24,28},{1,5},{5,9},{9,... | collective-permute-start | bytes 786440 | tf_op jit(solution)/shard_map/ppermute | solution.py:14
  23.6 6.8 %collective-permute-start = (f32[1]{0:T(128)}, f32[1]{0:T(128)}, u32[]{:S(2)}, u32[]{:S(2)}) collective-permute-start(f32[1]{0:T(128)} %bitcast.1), channel_id=1, source_target_pairs={{0,4},{4,8},{8,12},{12,16},{16,20},{20,24},{24,28},{1,5},{5,9},{9,... | collective-permute-start | bytes 20 | tf_op jit(solution)/shard_map/ppermute | solution.py:14
  27.6 25.3 %collective-permute-start.8 = (f32[1]{0:T(128)}, f32[1]{0:T(128)}, u32[]{:S(2)}, u32[]{:S(2)}) collective-permute-start(f32[1]{0:T(128)} %bitcast.1), channel_id=1, source_target_pairs={{4,0},{8,4},{12,8},{16,12},{20,16},{24,20},{28,24},{5,1},{9,5},{13... | collective-permute-start | bytes 20 | tf_op jit(solution)/shard_map/ppermute | solution.py:14
  30.4 5.0 %collective-permute-start.1 = (f32[1]{0:T(128)}, f32[1]{0:T(128)}, u32[]{:S(2)}, u32[]{:S(2)}) collective-permute-start(f32[1]{0:T(128)} %collective-permute-done), channel_id=1, source_target_pairs={{0,4},{4,8},{8,12},{12,16},{16,20},{20,24},{24,28},{1,5},{5,9},{9,... | collective-permute-start | bytes 20 | tf_op jit(solution)/shard_map/ppermute | solution.py:14
  36.8 39.8 %copy-start.3 = (f32[4,128]{1,0:T(4,128)S(1)}, f32[4,128]{1,0:T(4,128)}, u32[]{:S(2)}) copy-start(f32[4,128]{1,0:T(4,128)} %param.11) | copy-start | bytes 6148
  36.8 11.6 %collective-permute-start.6 = (f32[4,128,128]{2,1,0:T(8,128)S(1)}, f32[4,128,128]{2,1,0:T(8,128)S(1)}, u32[]{:S(2)}, u32[]{:S(2)}) collective-permute-start(f32[4,128,128]{2,1,0:T(8,128)S(1)} %fusion.14), channel_id=1, source_target_pairs={{0,8},{4,12},{8,16},{12,20},{16,24},{20,28},{1,9},{5,13},{9,17},{1... | collective-permute-start | bytes 786440 | tf_op jit(solution)/shard_map/ppermute | solution.py:14
  43.9 3.9 %collective-permute-start.2 = (f32[1]{0:T(128)}, f32[1]{0:T(128)}, u32[]{:S(2)}, u32[]{:S(2)}) collective-permute-start(f32[1]{0:T(128)} %select_n.117), channel_id=1, source_target_pairs={{0,8},{4,12},{8,16},{12,20},{16,24},{20,28},{1,9},{5,13},{9,17},{1... | collective-permute-start | bytes 20 | tf_op jit(solution)/shard_map/ppermute | solution.py:14
  48.4 27.6 %collective-permute-start.7 = (f32[4,128,128]{2,1,0:T(8,128)S(1)}, f32[4,128,128]{2,1,0:T(8,128)S(1)}, u32[]{:S(2)}, u32[]{:S(2)}) collective-permute-start(f32[4,128,128]{2,1,0:T(8,128)S(1)} %fusion.13), channel_id=1, source_target_pairs={{0,16},{4,20},{8,24},{12,28},{1,17},{5,21},{9,25},{13,29},{2,18},{... | collective-permute-start | bytes 786440 | tf_op jit(solution)/shard_map/ppermute | solution.py:14
  53.0 5.5 %collective-permute-start.9 = (f32[1]{0:T(128)}, f32[1]{0:T(128)}, u32[]{:S(2)}, u32[]{:S(2)}) collective-permute-start(f32[1]{0:T(128)} %collective-permute-done.8), channel_id=1, source_target_pairs={{4,0},{8,4},{12,8},{16,12},{20,16},{24,20},{28,24},{5,1},{9,5},{13... | collective-permute-start | bytes 20 | tf_op jit(solution)/shard_map/ppermute | solution.py:14
  59.8 8.3 %collective-permute-start.10 = (f32[1]{0:T(128)}, f32[1]{0:T(128)}, u32[]{:S(2)}, u32[]{:S(2)}) collective-permute-start(f32[1]{0:T(128)} %select_n.135), channel_id=1, source_target_pairs={{8,0},{12,4},{16,8},{20,12},{24,16},{28,20},{9,1},{13,5},{17,9},{2... | collective-permute-start | bytes 20 | tf_op jit(solution)/shard_map/ppermute | solution.py:14
  62.9 7.8 %collective-permute-start.3 = (f32[1]{0:T(128)}, f32[1]{0:T(128)}, u32[]{:S(2)}, u32[]{:S(2)}) collective-permute-start(f32[1]{0:T(128)} %select_n.118), channel_id=1, source_target_pairs={{0,16},{4,20},{8,24},{12,28},{1,17},{5,21},{9,25},{13,29},{2,18},{... | collective-permute-start | bytes 20 | tf_op jit(solution)/shard_map/ppermute | solution.py:14
  68.8 5.3 %collective-permute-start.11 = (f32[1]{0:T(128)}, f32[1]{0:T(128)}, u32[]{:S(2)}, u32[]{:S(2)}) collective-permute-start(f32[1]{0:T(128)} %select_n.136), channel_id=1, source_target_pairs={{16,0},{20,4},{24,8},{28,12},{17,1},{21,5},{25,9},{29,13},{18,2},{... | collective-permute-start | bytes 20 | tf_op jit(solution)/shard_map/ppermute | solution.py:14
  77.3 8.0 %collective-permute-start.12 = (f32[4,128,128]{1,2,0:T(8,128)S(1)}, f32[4,128,128]{1,2,0:T(8,128)S(1)}, u32[]{:S(2)}, u32[]{:S(2)}) collective-permute-start(f32[4,128,128]{1,2,0:T(8,128)S(1)} %multiply_bitcast_fusion), channel_id=1, source_target_pairs={{4,0},{8,4},{12,8},{16,12},{20,16},{24,20},{28,24},{5,1},{9,5},{13... | collective-permute-start | bytes 786440 | tf_op jit(solution)/shard_map/ppermute | solution.py:14
  81.6 7.6 %copy-start.1 = (bf16[4,256,256]{2,1,0:T(8,128)(2,1)}, bf16[4,256,256]{2,1,0:T(8,128)(2,1)S(1)}, u32[]{:S(2)}) copy-start(bf16[4,256,256]{2,1,0:T(8,128)(2,1)S(1)} %fusion.2) | copy-start | bytes 1572868
  85.3 9.2 %collective-permute-start.13 = (f32[4,128,128]{1,2,0:T(8,128)S(1)}, f32[4,128,128]{1,2,0:T(8,128)S(1)}, u32[]{:S(2)}, u32[]{:S(2)}) collective-permute-start(f32[4,128,128]{1,2,0:T(8,128)S(1)} %collective-permute-done.12), channel_id=1, source_target_pairs={{4,0},{8,4},{12,8},{16,12},{20,16},{24,20},{28,24},{5,1},{9,5},{13... | collective-permute-start | bytes 786440 | tf_op jit(solution)/shard_map/ppermute | solution.py:14
  94.5 43.5 %collective-permute-start.14 = (f32[4,128,128]{1,2,0:T(8,128)S(1)}, f32[4,128,128]{1,2,0:T(8,128)}, u32[]{:S(2)}, u32[]{:S(2)}) collective-permute-start(f32[4,128,128]{1,2,0:T(8,128)S(1)} %fusion.11), channel_id=1, source_target_pairs={{8,0},{12,4},{16,8},{20,12},{24,16},{28,20},{9,1},{13,5},{17,9},{2... | collective-permute-start | bytes 786440 | tf_op jit(solution)/shard_map/ppermute | solution.py:14
  97.4 60.9 %all-to-all-start = ((bf16[2,128,512]{1,2,0:T(8,128)(2,1)}), bf16[2,128,512]{1,2,0:T(8,128)(2,1)S(1)}, u32[]{:S(2)}, u32[]{:S(2)}) async-start(bf16[2,128,512]{1,2,0:T(8,128)(2,1)} %pad_maximum_fusion), calls=%async_computation | async-start | bytes 524288 | tf_op jit(solution)/shard_map/all_to_all | solution.py:87
  139.1 16.6 %collective-permute-start.15 = (f32[4,128,128]{1,2,0:T(8,128)S(1)}, f32[4,128,128]{1,2,0:T(8,128)S(1)}, u32[]{:S(2)}, u32[]{:S(2)}) collective-permute-start(f32[4,128,128]{1,2,0:T(8,128)S(1)} %fusion.10), channel_id=1, source_target_pairs={{16,0},{20,4},{24,8},{28,12},{17,1},{21,5},{25,9},{29,13},{18,2},{... | collective-permute-start | bytes 786440 | tf_op jit(solution)/shard_map/ppermute | solution.py:14
Sparse Core Ops, SparseCore 0:
  30.4 59.8 all-gather.1
